TPU v7x, 32 devices: a whole 2x2x4 slice. The times are simulated.
32 devices in a mesh: row: 8 (over y, x, core), col: 4 (over z).
Axes of the slice: x: 2, y: 2, z: 4, core: 2. Of those that a mesh axis runs over, the one named last changes fastest.
Arguments:
- operator: bfloat16 [36864, 36864], P('row', 'col'), may hold values from -0.046875 to 0.046875
- sketch_right: bfloat16 [36864, 384], P(('col', 'row')), may hold values from -6 to 6
- sketch_left: bfloat16 [36864, 576], P(('row', 'col')), may hold values from -6 to 6
Outputs:
- left_factor: bfloat16 [36864, 384], P('row')
- right_factor: bfloat16 [36864, 384], P(('col', 'row'))
All inputs are finite; a program needn't handle non-finite values.
Results may differ from a plain program's by a relative error of at most 0.0015.
Values may be sent and summed in bfloat16 or wider, within the bound.
A program may use at most 192 MiB of HBM per device.

v0:
```python
import math
import jax
import jax.numpy as jnp
from jax import lax
from jax.sharding import PartitionSpec as P

N = 36864
L = 576


def transposed_product(wide, sketch):
    contract = (((0,), (0,)), ((), ()))
    high_part = wide.astype(jnp.bfloat16)
    rest = wide - lax.optimization_barrier(high_part).astype(jnp.float32)
    middle_part = rest.astype(jnp.bfloat16)
    low_part = (rest - lax.optimization_barrier(middle_part).astype(jnp.float32)).astype(
        jnp.bfloat16
    )
    total = lax.dot_general(high_part, sketch, contract, preferred_element_type=jnp.float32)
    total = total + lax.dot_general(
        middle_part, sketch, contract, preferred_element_type=jnp.float32
    )
    return total + lax.dot_general(low_part, sketch, contract, preferred_element_type=jnp.float32)


def on_device(operator, sketch_right, sketch_left):
    right_rows = lax.all_gather(sketch_right, "row", axis=0, tiled=True)
    left_rows = lax.all_gather(sketch_left, "col", axis=0, tiled=True)
    contract = (((0,), (0,)), ((), ()))
    wide_piece = lax.psum_scatter(
        lax.dot_general(operator, left_rows, contract, preferred_element_type=jnp.float32),
        "row",
        scatter_dimension=0,
        tiled=True,
    )
    core_term = transposed_product(wide_piece, sketch_right)
    core = lax.psum(core_term, ("row", "col"))
    gram = jnp.dot(core.T, core, precision=lax.Precision.HIGHEST)
    lower = jnp.linalg.cholesky(gram)
    identity = jnp.eye(gram.shape[0], dtype=jnp.float32)
    inverse = jax.scipy.linalg.solve_triangular(lower, identity, lower=True).T
    ortho = jnp.dot(core, inverse, precision=lax.Precision.HIGHEST)
    right_factor = jnp.dot(wide_piece, ortho, precision=lax.Precision.HIGHEST).astype(jnp.bfloat16)
    factor = math.sqrt(N * L)
    image_piece = lax.psum_scatter(
        jnp.dot(operator, right_rows, preferred_element_type=jnp.float32),
        "col",
        scatter_dimension=0,
        tiled=True,
    )
    left_piece = (factor * jnp.dot(image_piece, inverse, precision=lax.Precision.HIGHEST)).astype(
        jnp.bfloat16
    )
    left_factor = lax.all_gather(left_piece, "col", axis=0, tiled=True)
    return (left_factor, right_factor)


def solution(mesh):
    in_specs = (P("row", "col"), P(("col", "row"), None), P(("row", "col"), None))
    out_specs = (P("row", None), P(("col", "row"), None))
    return jax.shard_map(
        on_device, mesh=mesh, in_specs=in_specs, out_specs=out_specs, check_vma=False
    )
```

profile of v0, /device:TPU:0, one launch (start us, length us, event | category | flops | bytes accessed | tf_op | source)
XLA Modules:
  0.0 705.0 jit_solution(1187567815735294535)
XLA Ops:
  7.2 0.0 all-gather.6.cloned.1.call-start
  7.2 0.7 all-gather.6.cloned.1.call-update
  7.9 0.0 reduce-scatter.5.cloned.1.call-start
  7.9 103.5 %all-gather.6.cloned.1.call-done = bf16[4608,576]{0,1:T(8,128)(2,1)} async-done(((bf16[1152,576]{0,1:T(8,128)(2,1)}), bf16[4608,576]{0,1:T(8,128)(2,1)}) %all-gather.6.cloned.1.call-update) | async-done | bytes 5308432 | tf_op jit(solution)/shard_map/all_gather | solution.py:28
  111.4 58.7 %fusion.30 = f32[9216,576]{0,1:T(8,128)} fusion(bf16[4608,576]{0,1:T(8,128)(2,1)} %all-gather.6.cloned.1.call-done, bf16[4608,9216]{1,0:T(8,128)(2,1)} %param.3), kind=kOutput, calls=%fused_computation.64 | convolution fusion | flops 48922361856 | bytes 111476736 | tf_op jit(solution)/shard_map/dot_general | solution.py:31
  170.1 0.0 reduce-scatter.5.cloned.1.call-update
  170.1 0.0 all-gather.4.cloned.1.call-start
  170.2 0.7 all-gather.4.cloned.1.call-update
  170.8 0.0 all-reduce.3.cloned.1.call-start
  170.9 135.0 %reduce-scatter.5.cloned.1.call-done = f32[1152,576]{0,1:T(8,128)} async-done(((f32[9216,576]{0,1:T(8,128)}), f32[1152,576]{0,1:T(8,128)}) %reduce-scatter.5.cloned.1.call-update) | async-done | bytes 2654224 | tf_op jit(solution)/shard_map/reduce_scatter | solution.py:30
  305.9 2.0 convert_element_type.26
  308.0 0.5 copy-done
  308.5 0.3 fusion.1
  308.8 0.9 copy-done.1
  309.7 0.9 fusion.28
  310.5 0.9 fusion.2
  311.5 1.8 fusion.3
  313.3 0.0 all-reduce.3.cloned.1.call-update
  313.3 0.0 reduce-scatter.3.cloned.1.call-start
  313.4 43.2 %all-gather.4.cloned.1.call-done = bf16[9216,384]{1,0:T(8,128)(2,1)} async-done(((bf16[1152,384]{1,0:T(8,128)(2,1)}), bf16[9216,384]{1,0:T(8,128)(2,1)}) %all-gather.4.cloned.1.call-update) | async-done | bytes 7077904 | tf_op jit(solution)/shard_map/all_gather | solution.py:27
  356.6 52.8 %fusion.27 = f32[4608,384]{1,0:T(8,128)} fusion(bf16[4608,9216]{1,0:T(8,128)(2,1)} %param.3, bf16[9216,384]{1,0:T(8,128)(2,1)} %all-gather.4.cloned.1.call-done), kind=kOutput, calls=%fused_computation.61 | convolution fusion | flops 32614907904 | bytes 99090432 | tf_op jit(solution)/shard_map/dot_general | solution.py:46
  409.4 0.5 all-gather.8.cloned.1.call-start
  410.0 0.9 fusion.11
  410.8 81.1 %all-reduce.3.cloned.1.call-done = f32[576,384]{1,0:T(8,128)} async-done(((f32[576,384]{1,0:T(8,128)}), f32[576,384]{1,0:T(8,128)}) %all-reduce.3.cloned.1.call-update) | async-done | bytes 884752 | tf_op jit(solution)/shard_map/psum | solution.py:37
  491.9 3.6 fusion.29
  495.5 1.1 copy.5
  496.6 1.1 fusion.4
  497.7 0.8 copy-done.5
  498.5 11.7 %cholesky.77 = f32[128,128]{1,0:T(8,128)S(1)} custom-call(f32[128,128]{1,0:T(8,128)S(1)} %cholesky.192), custom_call_target="Cholesky" | custom-call | tf_op jit(solution)/shard_map/jit(cholesky)/cholesky | solution.py:39
  510.3 9.8 %custom-call.23 = f32[1,128,128]{1,2,0:T(8,128)S(1)} custom-call(f32[1,128,128]{2,1,0:T(8,128)S(1)} %get-tuple-element.26), custom_call_target="InvertDiagBlocksLowerTriangular" | custom-call | tf_op jit(solution)/shard_map/jit(cholesky)/cholesky | solution.py:39
  520.1 1.2 constant_dynamic-update-slice_fusion.2
  521.3 1.2 convolution_subtract_fusion.2
  522.5 0.6 cholesky.196
  523.1 13.3 %cholesky.162 = f32[128,128]{1,0:T(8,128)} custom-call(f32[128,128]{1,0:T(8,128)} %cholesky.196), custom_call_target="Cholesky" | custom-call | tf_op jit(solution)/shard_map/jit(cholesky)/cholesky | solution.py:39
  536.4 1.5 select_reduce_fusion.1
  537.9 11.3 %custom-call.24 = f32[1,128,128]{1,2,0:T(8,128)} custom-call(f32[1,128,128]{2,1,0:T(8,128)} %get-tuple-element.23), custom_call_target="InvertDiagBlocksLowerTriangular" | custom-call | tf_op jit(solution)/shard_map/jit(cholesky)/cholesky | solution.py:39
  549.2 1.0 convolution_dynamic-update-slice_fusion
  550.2 1.1 convolution_subtract_fusion.3
  551.3 11.7 %cholesky.181 = f32[128,128]{1,0:T(8,128)S(1)} custom-call(f32[128,128]{1,0:T(8,128)S(1)} %convolution_subtract_fusion.3), custom_call_target="Cholesky" | custom-call | tf_op jit(solution)/shard_map/jit(cholesky)/cholesky | solution.py:39
  563.0 0.7 compare_reduce_fusion.1
  565.1 0.6 compare_reduce_fusion
  566.4 0.9 select_select_fusion
  567.3 10.7 %while.1 = (s32[]{:T(128)}, f32[384,384]{1,0:T(8,128)}, s32[3,2]{0,1:T(2,128)S(1)}, f32[3,128,128]{2,1,0:T(8,128)}, s32[]{:T(128)}) while((s32[]{:T(128)}, f32[384,384]{1,0:T(8,128)}, s32[3,2]{0,1:T(2,128)S(1)}, f32[3,128,128]{2,1,0:T(8,128)}, s32[]{:T(128)}) %tuple.29), condition=%wide.while_cond, body=%wide.while_body.sunk | while | flops 2 | bytes 132705 | solution.py:41
  567.3 0.1 constant_dynamic-slice_fusion.2
  567.3 0.6 fusion.51
  567.9 2.9 bitcast_dynamic-update-slice_fusion.2
  570.8 0.1 constant_dynamic-slice_fusion.2
  570.9 0.6 fusion.51
  571.5 2.9 bitcast_dynamic-update-slice_fusion.2
  574.4 0.1 constant_dynamic-slice_fusion.2
  574.5 0.6 fusion.51
  575.1 2.9 bitcast_dynamic-update-slice_fusion.2
  578.0 30.5 %custom-call.25 = f32[3,128,128]{1,2,0:T(8,128)S(1)} custom-call(f32[3,128,128]{2,1,0:T(8,128)} %get-tuple-element.9), custom_call_target="InvertDiagBlocksLowerTriangular" | custom-call | tf_op jit(solution)/shard_map/jit(_solve_triangular)/triangular_solve | solution.py:41
  608.5 0.3 fusion.9
  608.8 1.3 convolution_subtract_fusion.1
  610.2 0.4 fusion.18
  610.6 1.5 convolution_subtract_fusion
  612.1 1.9 fusion.16
  613.9 3.3 reduce-scatter.3.cloned.1.call-done
  617.3 5.9 fusion
  623.2 2.9 fusion.5
  626.1 6.7 convolution_convert_fusion
  632.9 60.9 %all-gather.8.cloned.1.call-done = bf16[4608,384]{1,0:T(8,128)(2,1)} async-done(((bf16[1152,384]{1,0:T(8,128)(2,1)}), bf16[4608,384]{1,0:T(8,128)(2,1)}) %all-gather.8.cloned.1.call-update) | async-done | bytes 3538960 | tf_op jit(solution)/shard_map/all_gather | solution.py:54
  693.8 4.1 copy.22
  (21 shorter events, 0.2 us)
Async XLA Ops:
  7.2 104.3 %all-gather.6.cloned.1.call-start = ((), (), s32[]{:S(2)}) async-start(), calls=%async_computation.4 | async-start | bytes 6635520 | tf_op jit(solution)/shard_map/all_gather | solution.py:28
  7.9 298.0 %reduce-scatter.5.cloned.1.call-start = ((), (), s32[]{:S(2)}) async-start(), calls=%async_computation.5 | async-start | bytes 23887872 | tf_op jit(solution)/shard_map/reduce_scatter | solution.py:30
  170.1 186.5 %all-gather.4.cloned.1.call-start = ((), (), s32[]{:S(2)}) async-start(), calls=%async_computation.2 | async-start | bytes 7962624 | tf_op jit(solution)/shard_map/all_gather | solution.py:27
  170.8 321.0 %all-reduce.3.cloned.1.call-start = ((), (), s32[]{:S(2)}) async-start(), calls=%async_computation.6 | async-start | bytes 1769472 | tf_op jit(solution)/shard_map/psum | solution.py:37
  305.9 2.5 copy-start
  308.5 1.2 copy-start.1
  313.3 304.0 %reduce-scatter.3.cloned.1.call-start = ((), (), s32[]{:S(2)}) async-start(), calls=%async_computation.3 | async-start | bytes 8847360 | tf_op jit(solution)/shard_map/reduce_scatter | solution.py:45
  409.4 284.4 %all-gather.8.cloned.1.call-start = ((), (), s32[]{:S(2)}) async-start(), calls=%async_computation.7 | async-start | bytes 4423680 | tf_op jit(solution)/shard_map/all_gather | solution.py:54
  497.7 0.8 copy-start.5
  608.5 1.7 copy-start.6
  608.8 1.8 copy-start.3
  610.5 1.5 copy-start.4
  610.6 12.6 %copy-start.2 = (f32[576,384]{1,0:T(8,128)S(1)}, f32[576,384]{1,0:T(8,128)}, u32[]{:S(2)}) copy-start(f32[576,384]{1,0:T(8,128)} %all-reduce.3.cloned.1.call-done) | copy-start | bytes 2654212
Sparse Core Ops, SparseCore 0:
  9.5 101.8 all-gather.5
  170.2 135.6 reduce-scatter.4
  307.8 48.6 all-gather.3
  362.2 129.6 all-reduce.2
  494.0 123.1 reduce-scatter.2
  623.3 70.4 all-gather.7
where the time goes:
time: 713 us; the launch traced here: 705 us
  waiting for transfers between devices  428 us (60%)
  matrix products  144 us (20%)
  other arithmetic  96.4 us (14%)
  local copies, waits for them, and re-layouts  18.8 us (3%)
  between operations  16.5 us (2%)
    reduce_scatter x1, waiting for transfers between devices, on_device(): lax.psum_scatter(lax.dot_general(operator, left_rows, contract, preferred...  135 us
    all_gather x1, waiting for transfers between devices, on_device(): left_rows = lax.all_gather(sketch_left, 'col', axis=0, tiled=True)  103 us
    psum x1, waiting for transfers between devices, on_device(): core = lax.psum(core_term, ('row', 'col'))  81.1 us
    all_gather x1, waiting for transfers between devices, on_device(): left_factor = lax.all_gather(left_piece, 'col', axis=0, tiled=True)  60.9 us
    another operation x10, other arithmetic, on_device(): lower = jnp.linalg.cholesky(gram)  60.7 us
    dot_general x1, matrix products, on_device(): lax.dot_general(operator, left_rows, contract, preferred_element_type=jnp...  58.7 us
    dot_general x1, matrix products, on_device(): jnp.dot(operator, right_rows, preferred_element_type=jnp.float32)  52.8 us
    all_gather x1, waiting for transfers between devices, on_device(): right_rows = lax.all_gather(sketch_right, 'row', axis=0, tiled=True)  43.2 us
  transfers between devices with their start and end apart: 6, of which 6 were waited for; matrix products, arithmetic and copies ran while one was open for 27% of the time, Pallas kernels for 0%

commit v1 on v0

--- a/solution.py
+++ b/solution.py
@@ -25,7 +25,12 @@
 
 def on_device(operator, sketch_right, sketch_left):
     right_rows = lax.all_gather(sketch_right, "row", axis=0, tiled=True)
-    left_rows = lax.all_gather(sketch_left, "col", axis=0, tiled=True)
+    ring = [sketch_left]
+    for hop in range(3):
+        ring.append(lax.ppermute(ring[-1], "col", [(dev, (dev + 1) % 4) for dev in range(4)]))
+    left_rows = jnp.roll(
+        jnp.concatenate(ring[::-1], axis=0), (lax.axis_index("col") + 1) * ring[0].shape[0], axis=0
+    )
     contract = (((0,), (0,)), ((), ()))
     wide_piece = lax.psum_scatter(
         lax.dot_general(operator, left_rows, contract, preferred_element_type=jnp.float32),

time: 713 us -> 720 us (level)
  waiting for transfers between devices: 428 us -> 408 us
  starting transfers between devices: 0.7 us -> 14.5 us
  local copies, waits for them, and re-layouts: 18.8 us -> 32.1 us
    all_gather x1 -> x0, waiting for transfers between devices: 103 us -> none  [on_device(): left_rows = lax.all_gather(sketch_left, 'col', axis=0, tiled=True)]
    ppermute x0 -> x3, waiting for transfers between devices: none -> 94.8 us  [on_device(): lax.ppermute(ring[-1], 'col', [(dev, (dev + 1) % 4) for dev in range(4)])]
    unnamed x15 -> x28, local copies, waits for them, and re-layouts: 6.35 us -> 19 us
    all_gather x1, waiting for transfers between devices: 43.2 us -> 32 us  [on_device(): right_rows = lax.all_gather(sketch_right, 'row', axis=0, tiled=True)]
    reduce_scatter x1, starting transfers between devices: 0.04 us -> 11.3 us  [on_device(): lax.psum_scatter(jnp.dot(operator, right_rows, preferred_element_type=jnp...]
  transfers between devices with their start and end apart: 6 -> 8, of which waited for: 6 -> 8; matrix products, arithmetic and copies ran while one was open for 27% -> 26% of each run, Pallas kernels for 0% -> 0%
where the time goes in v1:
time: 720 us; the launch traced here: 712 us
  waiting for transfers between devices  408 us (57%)
  matrix products  145 us (20%)
  other arithmetic  96.6 us (13%)
  local copies, waits for them, and re-layouts  32.1 us (4%)
  between operations  16.1 us (2%)
  starting transfers between devices  14.5 us (2%)
    reduce_scatter x1, waiting for transfers between devices, on_device(): lax.psum_scatter(lax.dot_general(operator, left_rows, contract, preferred...  134 us
    ppermute x3, waiting for transfers between devices, on_device(): lax.ppermute(ring[-1], 'col', [(dev, (dev + 1) % 4) for dev in range(4)])  94.8 us
    psum x1, waiting for transfers between devices, on_device(): core = lax.psum(core_term, ('row', 'col'))  81.7 us
    another operation x10, other arithmetic, on_device(): lower = jnp.linalg.cholesky(gram)  60.9 us
    all_gather x1, waiting for transfers between devices, on_device(): left_factor = lax.all_gather(left_piece, 'col', axis=0, tiled=True)  60.9 us
    dot_general x1, matrix products, on_device(): lax.dot_general(operator, left_rows, contract, preferred_element_type=jnp...  59.1 us
    dot_general x1, matrix products, on_device(): jnp.dot(operator, right_rows, preferred_element_type=jnp.float32)  52.8 us
    all_gather x1, waiting for transfers between devices, on_device(): right_rows = lax.all_gather(sketch_right, 'row', axis=0, tiled=True)  32 us
  transfers between devices with their start and end apart: 8, of which 8 were waited for; matrix products, arithmetic and copies ran while one was open for 26% of the time, Pallas kernels for 0%

profile of v1, /device:TPU:0, one launch (start us, length us, event | category | flops | bytes accessed | tf_op | source)
XLA Modules:
  0.0 712.3 jit_solution(3542221852939207512)
XLA Ops:
  7.2 3.1 collective-permute-start
  10.3 31.4 %collective-permute-done = bf16[1152,576]{0,1:T(8,128)(2,1)S(1)} collective-permute-done((bf16[1152,576]{0,1:T(8,128)(2,1)}, bf16[1152,576]{0,1:T(8,128)(2,1)S(1)}, u32[]{:S(2)}, u32[]{:S(2)}) %collective-permute-start) | collective-permute-done | bytes 1327136 | tf_op jit(solution)/shard_map/ppermute | solution.py:30
  41.7 32.1 %collective-permute-done.1 = bf16[1152,576]{0,1:T(8,128)(2,1)S(1)} collective-permute-done((bf16[1152,576]{0,1:T(8,128)(2,1)S(1)}, bf16[1152,576]{0,1:T(8,128)(2,1)S(1)}, u32[]{:S(2)}, u32[]{:S(2)}) %collective-permute-start.1) | collective-permute-done | bytes 1327136 | tf_op jit(solution)/shard_map/ppermute | solution.py:30
  73.8 31.3 %collective-permute-done.2 = bf16[1152,576]{0,1:T(8,128)(2,1)} collective-permute-done((bf16[1152,576]{0,1:T(8,128)(2,1)S(1)}, bf16[1152,576]{0,1:T(8,128)(2,1)}, u32[]{:S(2)}, u32[]{:S(2)}) %collective-permute-start.2) | collective-permute-done | bytes 1327136 | tf_op jit(solution)/shard_map/ppermute | solution.py:30
  105.1 2.5 constant_dynamic-update-slice_fusion.7
  107.6 2.6 constant_dynamic-update-slice_fusion.6
  110.3 1.3 constant_dynamic-update-slice_fusion.5
  111.5 1.2 constant_dynamic-update-slice_fusion.4
  112.7 2.5 constant_dynamic-update-slice_fusion.3
  115.3 1.3 constant_dynamic-update-slice_fusion.2
  116.5 1.2 constant_dynamic-update-slice_fusion.1
  117.8 1.2 constant_dynamic-update-slice_fusion
  119.0 59.1 %convolution_bitcast_fusion = f32[9216,576]{0,1:T(8,128)} fusion(bf16[4608,9216]{1,0:T(8,128)(2,1)} %param.3, bf16[9216,576]{0,1:T(8,128)(2,1)} %constant_dynamic-update-slice_fusion, s32[]{:T(128)S(6)} %select_n.18), kind=kOutput, calls=%fused_computation.2 | convolution fusion | flops 48922361856 | bytes 111476736 | tf_op jit(solution)/shard_map/dot_general | solution.py:36
  178.2 0.7 all-gather.3.cloned.1.call-update
  178.9 134.5 %reduce-scatter.5.cloned.1.call-done = f32[1152,576]{0,1:T(8,128)} async-done(((f32[9216,576]{0,1:T(8,128)}), f32[1152,576]{0,1:T(8,128)}) %reduce-scatter.5.cloned.1.call-update) | async-done | bytes 2654224 | tf_op jit(solution)/shard_map/reduce_scatter | solution.py:35
  313.4 2.0 convert_element_type.26
  315.5 0.5 copy-done
  316.0 0.3 fusion.2
  316.3 0.9 copy-done.1
  317.1 0.9 fusion.30
  318.0 0.9 fusion.3
  318.9 1.8 fusion.4
  320.8 11.3 %reduce-scatter.3.cloned.1.call-start = ((), (), s32[]{:S(2)}) async-start(), calls=%async_computation.3 | async-start | bytes 8847360 | tf_op jit(solution)/shard_map/reduce_scatter | solution.py:50
  332.1 32.0 %all-gather.3.cloned.1.call-done = bf16[9216,384]{1,0:T(8,128)(2,1)} async-done(((bf16[1152,384]{1,0:T(8,128)(2,1)}), bf16[9216,384]{1,0:T(8,128)(2,1)}) %all-gather.3.cloned.1.call-update) | async-done | bytes 7077904 | tf_op jit(solution)/shard_map/all_gather | solution.py:27
  364.1 52.8 %fusion.29 = f32[4608,384]{1,0:T(8,128)} fusion(bf16[4608,9216]{1,0:T(8,128)(2,1)} %param.3, bf16[9216,384]{1,0:T(8,128)(2,1)} %all-gather.3.cloned.1.call-done), kind=kOutput, calls=%fused_computation.72 | convolution fusion | flops 32614907904 | bytes 99090432 | tf_op jit(solution)/shard_map/dot_general | solution.py:51
  417.0 0.9 fusion.12
  417.8 81.7 %all-reduce.3.cloned.1.call-done = f32[576,384]{1,0:T(8,128)} async-done(((f32[576,384]{1,0:T(8,128)}), f32[576,384]{1,0:T(8,128)}) %all-reduce.3.cloned.1.call-update) | async-done | bytes 884752 | tf_op jit(solution)/shard_map/psum | solution.py:42
  499.5 3.6 fusion.31
  503.1 1.1 copy.5
  504.2 1.1 fusion.5
  505.3 0.8 copy-done.8
  506.1 11.7 %cholesky.77 = f32[128,128]{1,0:T(8,128)S(1)} custom-call(f32[128,128]{1,0:T(8,128)S(1)} %cholesky.192), custom_call_target="Cholesky" | custom-call | tf_op jit(solution)/shard_map/jit(cholesky)/cholesky | solution.py:44
  517.9 9.8 %custom-call.23 = f32[1,128,128]{1,2,0:T(8,128)S(1)} custom-call(f32[1,128,128]{2,1,0:T(8,128)S(1)} %get-tuple-element.26), custom_call_target="InvertDiagBlocksLowerTriangular" | custom-call | tf_op jit(solution)/shard_map/jit(cholesky)/cholesky | solution.py:44
  527.7 1.2 constant_dynamic-update-slice_fusion.10
  528.9 1.2 convolution_subtract_fusion.2
  530.1 0.6 cholesky.196
  530.7 13.6 %cholesky.162 = f32[128,128]{1,0:T(8,128)} custom-call(f32[128,128]{1,0:T(8,128)} %cholesky.196), custom_call_target="Cholesky" | custom-call | tf_op jit(solution)/shard_map/jit(cholesky)/cholesky | solution.py:44
  544.3 1.5 select_reduce_fusion.1
  545.8 11.3 %custom-call.24 = f32[1,128,128]{1,2,0:T(8,128)} custom-call(f32[1,128,128]{2,1,0:T(8,128)} %get-tuple-element.23), custom_call_target="InvertDiagBlocksLowerTriangular" | custom-call | tf_op jit(solution)/shard_map/jit(cholesky)/cholesky | solution.py:44
  557.0 1.0 convolution_dynamic-update-slice_fusion
  558.1 1.1 convolution_subtract_fusion.3
  559.2 11.7 %cholesky.181 = f32[128,128]{1,0:T(8,128)S(1)} custom-call(f32[128,128]{1,0:T(8,128)S(1)} %convolution_subtract_fusion.3), custom_call_target="Cholesky" | custom-call | tf_op jit(solution)/shard_map/jit(cholesky)/cholesky | solution.py:44
  570.9 0.7 compare_reduce_fusion.1
  572.9 0.6 compare_reduce_fusion
  574.2 0.9 select_select_fusion
  575.1 10.2 %while.1 = (s32[]{:T(128)}, f32[384,384]{1,0:T(8,128)}, s32[3,2]{0,1:T(2,128)S(1)}, f32[3,128,128]{2,1,0:T(8,128)}, s32[]{:T(128)}) while((s32[]{:T(128)}, f32[384,384]{1,0:T(8,128)}, s32[3,2]{0,1:T(2,128)S(1)}, f32[3,128,128]{2,1,0:T(8,128)}, s32[]{:T(128)}) %tuple.29), condition=%wide.while_cond, body=%wide.while_body.sunk | while | flops 2 | bytes 132705 | solution.py:46
  575.1 0.5 fusion.54
  575.7 2.8 bitcast_dynamic-update-slice_fusion.2
  578.6 0.5 fusion.54
  579.1 2.8 bitcast_dynamic-update-slice_fusion.2
  582.0 0.5 fusion.54
  582.5 2.7 bitcast_dynamic-update-slice_fusion.2
  585.3 30.5 %custom-call.25 = f32[3,128,128]{1,2,0:T(8,128)S(1)} custom-call(f32[3,128,128]{2,1,0:T(8,128)} %get-tuple-element.9), custom_call_target="InvertDiagBlocksLowerTriangular" | custom-call | tf_op jit(solution)/shard_map/jit(_solve_triangular)/triangular_solve | solution.py:46
  615.8 0.3 fusion.10
  616.1 1.3 convolution_subtract_fusion.1
  617.5 0.4 fusion.19
  617.9 1.5 convolution_subtract_fusion
  619.4 1.9 fusion.17
  621.2 3.7 reduce-scatter.3.cloned.1.call-done
  625.0 5.9 fusion.1
  630.9 2.9 fusion.6
  633.8 6.7 convolution_convert_fusion
  640.5 60.9 %all-gather.5.cloned.1.call-done = bf16[4608,384]{1,0:T(8,128)(2,1)} async-done(((bf16[1152,384]{1,0:T(8,128)(2,1)}), bf16[4608,384]{1,0:T(8,128)(2,1)}) %all-gather.5.cloned.1.call-update) | async-done | bytes 3538960 | tf_op jit(solution)/shard_map/all_gather | solution.py:59
  701.4 4.1 copy.29
  (38 shorter events, 0.7 us)
Async XLA Ops:
  7.2 306.3 %reduce-scatter.5.cloned.1.call-start = ((), (), s32[]{:S(2)}) async-start(), calls=%async_computation.4 | async-start | bytes 23887872 | tf_op jit(solution)/shard_map/reduce_scatter | solution.py:35
  7.2 34.5 %collective-permute-start = (bf16[1152,576]{0,1:T(8,128)(2,1)}, bf16[1152,576]{0,1:T(8,128)(2,1)S(1)}, u32[]{:S(2)}, u32[]{:S(2)}) collective-permute-start(bf16[1152,576]{0,1:T(8,128)(2,1)} %param.5), channel_id=1, source_target_pairs={{0,1},{1,2},{2,3},{3,0},{4,5},{5,6},{6,7},{7,4},{8,9},{9,10},{10,1... | collective-permute-start | bytes 3981320 | tf_op jit(solution)/shard_map/ppermute | solution.py:30
  41.7 32.1 %collective-permute-start.1 = (bf16[1152,576]{0,1:T(8,128)(2,1)S(1)}, bf16[1152,576]{0,1:T(8,128)(2,1)S(1)}, u32[]{:S(2)}, u32[]{:S(2)}) collective-permute-start(bf16[1152,576]{0,1:T(8,128)(2,1)S(1)} %collective-permute-done), channel_id=1, source_target_pairs={{0,1},{1,2},{2,3},{3,0},{4,5},{5,6},{6,7},{7,4},{8,9},{9,10},{10,1... | collective-permute-start | bytes 3981320 | tf_op jit(solution)/shard_map/ppermute | solution.py:30
  73.8 31.3 %copy-start.4 = (bf16[1152,576]{0,1:T(8,128)(2,1)}, bf16[1152,576]{0,1:T(8,128)(2,1)S(1)}, u32[]{:S(2)}) copy-start(bf16[1152,576]{0,1:T(8,128)(2,1)S(1)} %collective-permute-done.1) | copy-start | bytes 3981316
  73.8 31.3 %collective-permute-start.2 = (bf16[1152,576]{0,1:T(8,128)(2,1)S(1)}, bf16[1152,576]{0,1:T(8,128)(2,1)}, u32[]{:S(2)}, u32[]{:S(2)}) collective-permute-start(bf16[1152,576]{0,1:T(8,128)(2,1)S(1)} %collective-permute-done.1), channel_id=1, source_target_pairs={{0,1},{1,2},{2,3},{3,0},{4,5},{5,6},{6,7},{7,4},{8,9},{9,10},{10,1... | collective-permute-start | bytes 3981320 | tf_op jit(solution)/shard_map/ppermute | solution.py:30
  107.6 3.9 copy-start.3
  111.5 3.8 copy-start.5
  178.1 185.9 %all-gather.3.cloned.1.call-start = ((), (), s32[]{:S(2)}) async-start(), calls=%async_computation.2 | async-start | bytes 7962624 | tf_op jit(solution)/shard_map/all_gather | solution.py:27
  178.9 320.6 %all-reduce.3.cloned.1.call-start = ((), (), s32[]{:S(2)}) async-start(), calls=%async_computation.5 | async-start | bytes 1769472 | tf_op jit(solution)/shard_map/psum | solution.py:42
  313.4 2.5 copy-start
  316.0 1.2 copy-start.1
  320.8 304.2 %reduce-scatter.3.cloned.1.call-start = ((), (), s32[]{:S(2)}) async-start(), calls=%async_computation.3 | async-start | bytes 8847360 | tf_op jit(solution)/shard_map/reduce_scatter | solution.py:50
  416.9 284.5 %all-gather.5.cloned.1.call-start = ((), (), s32[]{:S(2)}) async-start(), calls=%async_computation.6 | async-start | bytes 4423680 | tf_op jit(solution)/shard_map/all_gather | solution.py:59
  505.3 0.8 copy-start.8
  615.8 1.7 copy-start.9
  616.1 1.8 copy-start.6
  617.8 1.5 copy-start.7
  617.9 13.0 %copy-start.2 = (f32[576,384]{1,0:T(8,128)S(1)}, f32[576,384]{1,0:T(8,128)}, u32[]{:S(2)}) copy-start(f32[576,384]{1,0:T(8,128)} %all-reduce.3.cloned.1.call-done) | copy-start | bytes 2654212
Sparse Core Ops, SparseCore 0:
  178.2 135.1 reduce-scatter.4
  315.3 48.6 all-gather.2
  369.9 129.6 all-reduce.2
  501.7 123.2 reduce-scatter.2
  631.0 70.3 all-gather.4
